TPU v7x, 32 devices: a whole 2x2x4 slice. The times are simulated.
32 devices in a mesh: groups: 2 (over y), seq: 8 (over z, x), section: 2 (over core).
Axes of the slice: x: 2, y: 2, z: 4, core: 2. Of those that a mesh axis runs over, the one named last changes fastest.
Arguments:
- skip_in: bfloat16 [2, 1024, 1536], P('groups', 'seq'), parts along dimension 0, may hold values from -6 to 6
- attn_gain: float32 [1536], replicated, may hold values from 0.25 to 1.75
- query_weight: bfloat16 [1536, 1024], P(None, 'section'), may hold values from -0.625 to 0.625
- kv_weight: bfloat16 [1536, 256], replicated, may hold values from -0.15625 to 0.15625
- pair_bias: float32 [2, 8, 32, 32], P('groups', 'section', 'seq'), parts along dimension 0, may hold values from -12 to 400
- out_weight: bfloat16 [1024, 1536], P('section'), may hold values from -0.1875 to 0.1875
- dec_gain: float32 [1536], replicated, may hold values from 0.25 to 1.75
- dec_weight: bfloat16 [5, 1536, 768], P(None, 'seq', 'section'), may hold values from -0.0625 to 0.0625
- dec_bias: float32 [768], P('section'), may hold values from -3 to 3
Outputs:
- decoded: bfloat16 [2, 1024, 768], P('groups', 'seq', 'section'), parts along dimension 0
There are 2 independent parts, one for each index of `groups`. A program takes and returns all parts, laid end to end along the dimension named above; an argument that names none is the same for every part. Nothing has to cross between parts.
All inputs are finite; a program needn't handle non-finite values.
Results may differ from a plain program's by a relative error of at most 0.0095.
Values may be sent and summed in bfloat16 or wider, within the bound.
No kernel may reach another device: no remote copies, remote signals or barrier semaphores. Data moves between devices by JAX's collectives and lax.ppermute only.
A program may use at most 64 MiB of HBM per device.

v0:
```python
import math
import jax
import jax.numpy as jnp
from jax import lax
from jax.sharding import PartitionSpec as P

HEAD = 128
KW = 5
PAIR = 16


def extended(block, sides, width):
    for axis, dim in sides:
        count = lax.axis_size(axis)
        forward = [(i, i + 1) for i in range(count - 1)]
        backward = [(target, source) for source, target in forward]
        low = lax.ppermute(
            lax.slice_in_dim(block, block.shape[dim] - width, None, axis=dim), axis, forward
        )
        high = lax.ppermute(lax.slice_in_dim(block, 0, width, axis=dim), axis, backward)
        block = jnp.concatenate([low, block, high], axis=dim)
    return block


def norm_scale(values_in, gain):
    wide = values_in.astype(jnp.float32)
    return wide * lax.rsqrt(jnp.mean(wide * wide, axis=-1, keepdims=True) + 1e-06) * gain


def body(
    skip_in,
    attn_gain,
    query_weight,
    kv_weight,
    pair_bias,
    out_weight,
    dec_gain,
    dec_weight,
    dec_bias,
):
    seq_count, local_rows, channels = skip_in.shape
    half_rows = local_rows // 2
    local_heads = query_weight.shape[1] // HEAD
    logit_scale = 1.0 / math.sqrt(HEAD)
    pooled = jnp.max(skip_in.reshape(seq_count, half_rows, 2, channels), axis=2)
    normed = norm_scale(pooled, attn_gain).astype(jnp.bfloat16)
    flattened = normed.reshape(seq_count * half_rows, channels)
    query_rows = jnp.dot(flattened, query_weight, preferred_element_type=jnp.float32).astype(
        jnp.bfloat16
    )
    query_rows = query_rows.reshape(seq_count, half_rows, local_heads, HEAD)
    row_bias = jnp.repeat(pair_bias, PAIR, axis=2)
    row_bias = jnp.pad(row_bias, ((0, 0), (0, 0), (0, 0), (0, 2)))
    quarter = half_rows // 2
    own_rows = lax.dynamic_slice_in_dim(normed, lax.axis_index("section") * quarter, quarter, 1)
    key_values = jnp.dot(
        own_rows.reshape(seq_count * quarter, channels),
        kv_weight,
        preferred_element_type=jnp.float32,
    )
    key_values = key_values.astype(jnp.bfloat16).reshape(seq_count, quarter, 2 * HEAD)
    piece = lax.all_gather(key_values, ("seq", "section"), axis=1, tiled=True)
    start = jnp.int32(0)
    running_max = jnp.full((seq_count, local_heads, half_rows), -1e30, jnp.float32)
    running_sum = jnp.zeros((seq_count, local_heads, half_rows), jnp.float32)
    weighted = jnp.zeros((seq_count, local_heads, half_rows, HEAD), jnp.float32)
    piece_rows = piece.shape[1]
    block_size = min(piece_rows, 2048)
    for offset in range(0, piece_rows, block_size):
        piece_len = min(block_size, piece_rows - offset)
        sub_piece = piece[:, offset : offset + piece_len]
        key_portion = sub_piece[:, :, :HEAD]
        value_part = sub_piece[:, :, HEAD:]
        first_row = start + offset
        blocks = lax.dynamic_slice_in_dim(row_bias, first_row // PAIR, piece_len // PAIR + 2, 3)
        spread = jnp.repeat(blocks, PAIR, axis=3)
        key_bias = lax.dynamic_slice_in_dim(spread, first_row % PAIR, piece_len, 3)
        scores = (
            jnp.einsum(
                "wtzj,wgj->wztg", query_rows, key_portion, preferred_element_type=jnp.float32
            )
            * logit_scale
            + key_bias
        )
        new_max = jnp.maximum(running_max, jnp.max(scores, axis=-1))
        rescale = jnp.exp(running_max - new_max)
        exponent_scores = jnp.exp(scores - new_max[..., None])
        running_sum = running_sum * rescale + jnp.sum(exponent_scores, axis=-1)
        weighted = weighted * rescale[..., None] + jnp.einsum(
            "umrl,ult->umrt",
            exponent_scores.astype(jnp.bfloat16),
            value_part,
            preferred_element_type=jnp.float32,
        )
        running_max = new_max
    folded = (running_max, running_sum, weighted)
    running_max, running_sum, weighted = folded
    context = (weighted / running_sum[..., None]).astype(jnp.bfloat16)
    context = jnp.transpose(context, (0, 2, 1, 3)).reshape(
        seq_count * half_rows, local_heads * HEAD
    )
    partial_value = jnp.dot(context, out_weight, preferred_element_type=jnp.float32).reshape(
        seq_count, half_rows, channels
    )
    summed = lax.psum(partial_value.astype(jnp.bfloat16), "section").astype(jnp.float32)
    attended = (pooled.astype(jnp.float32) + summed).astype(jnp.bfloat16)
    joined = (
        jnp.repeat(attended, 2, axis=1).astype(jnp.float32) + skip_in.astype(jnp.float32)
    ).astype(jnp.bfloat16)
    activated = jax.nn.gelu(norm_scale(joined, dec_gain)).astype(jnp.bfloat16)
    padded = extended(activated, (("seq", 1),), KW // 2)
    out_half = dec_weight.shape[2]
    piece = lax.all_gather(dec_weight, "seq", axis=1, tiled=True)
    piece_rows = piece.shape[1]
    stacked = jnp.concatenate(
        [padded[:, tap_index : tap_index + local_rows] for tap_index in range(KW)], axis=2
    )
    stacked = stacked.reshape(seq_count * local_rows, KW * piece_rows)
    convolved = jnp.dot(
        stacked, piece.reshape(KW * piece_rows, out_half), preferred_element_type=jnp.float32
    )
    residual = lax.dynamic_slice_in_dim(joined, lax.axis_index("section") * out_half, out_half, 2)
    decoded = (
        convolved.reshape(seq_count, local_rows, out_half) + dec_bias + residual.astype(jnp.float32)
    )
    return decoded.astype(jnp.bfloat16)


def solution(mesh):
    return jax.shard_map(
        body,
        mesh=mesh,
        in_specs=(
            P("groups", "seq", None),
            P(),
            P(None, "section"),
            P(),
            P("groups", "section", "seq", None),
            P("section", None),
            P(),
            P(None, "seq", "section"),
            P("section"),
        ),
        out_specs=P("groups", "seq", "section"),
        check_vma=False,
    )
```

profile of v0, /device:TPU:0, one launch (start us, length us, event | category | flops | bytes accessed | tf_op | source)
XLA Modules:
  0.0 150.7 jit_solution(8483585687084230014)
XLA Ops:
  7.4 0.0 copy-start
  7.4 0.0 copy-start.2
  7.4 0.0 copy-start.1
  7.4 0.0 all-reduce.3.cloned.1.call-start
  7.4 2.0 %reshape.220 = bf16[64,2,1536]{2,1,0:T(2,128)(2,1)} reshape(bf16[1,128,1536]{2,1,0:T(8,128)(2,1)} %param.9) | data formatting | bytes 786432 | tf_op jit(solution)/shard_map/reshape | solution.py:45
  9.4 2.0 %reduce_max.18 = bf16[64,1536]{1,0:T(8,128)(2,1)S(1)} reduce(bf16[64,2,1536]{2,1,0:T(2,128)(2,1)} %reshape.220, bf16[]{:T(256)} %constant.24.clone.1), dimensions={1}, to_apply=%region_0.0 | reduce | flops 98304 | bytes 589826 | tf_op jit(solution)/shard_map/reduce_max | solution.py:45
  11.4 0.0 copy-start.4
  11.4 0.1 fusion.37
  11.5 0.8 convert_bitcast_fusion
  12.3 0.1 dynamic-slice.1
  12.4 0.0 copy-done.2
  12.4 1.5 %convolution_convert_fusion.2 = bf16[32,256]{1,0:T(8,128)(2,1)S(1)} fusion(bf16[1536,256]{1,0:T(8,128)(2,1)} %param.12, f32[1,64,1536]{2,1,0:T(8,128)} %convert_bitcast_fusion, s32[]{:T(128)S(6)} %select_n.15, f32[1536]{0:T(1024)S(1)} %copy-done.2, f32[32]{0:T(128)S(1)} %dynamic-slice.1), kind=kOutput, calls=%fused_computation.18 | convolution fusion | flops 25321472 | bytes 1005700 | tf_op jit(solution)/shard_map/dot_general | solution.py:56
  13.9 25.2 %all-gather = bf16[512,256]{1,0:T(8,128)(2,1)} all-gather(bf16[32,256]{1,0:T(8,128)(2,1)S(1)} %convolution_convert_fusion.2), channel_id=2, replica_groups=mesh['groups'=2,'seq'=8,'section'=2] {'seq','section'}, dimensions={0}, use_global_device_ids=true | all-gather | bytes 278528 | tf_op jit(solution)/shard_map/all_gather | solution.py:62
  39.1 0.0 copy-done.1
  39.1 0.4 fusion.19
  39.6 0.0 copy-done.4
  39.6 0.1 copy.16
  39.7 0.1 broadcast_in_dim.31
  39.8 0.1 slice.41
  39.9 0.3 copy.19
  40.2 1.2 fusion.63
  41.4 0.2 fusion.31
  41.7 1.2 fusion.20
  42.9 0.1 copy.18
  42.9 0.0 copy-done
  42.9 1.1 fusion
  44.0 0.0 all-reduce.3.cloned.1.call-update
  44.0 0.0 all-gather.3.cloned.1.call-start
  44.1 0.5 all-gather.3.cloned.1.call-update
  44.6 15.0 %all-reduce.3.cloned.1.call-done = bf16[1,64,1536]{2,1,0:T(8,128)(2,1)} async-done(((bf16[1,64,1536]{2,1,0:T(8,128)(2,1)}), bf16[1,64,1536]{2,1,0:T(8,128)(2,1)}) %all-reduce.3.cloned.1.call-update) | async-done | bytes 196624 | tf_op jit(solution)/shard_map/psum | solution.py:105
  59.6 1.0 fusion.46
  60.6 0.0 copy-start.3
  60.6 0.3 broadcast_in_dim.34
  60.9 0.5 convert_element_type.120
  61.4 1.2 fusion.21
  62.6 0.0 copy-done.3
  62.6 0.4 fusion.25
  63.0 3.6 %collective-permute-start = (bf16[1,2,1536]{2,1,0:T(2,128)(2,1)S(1)}, bf16[1,2,1536]{2,1,0:T(2,128)(2,1)S(1)}, u32[]{:S(2)}, u32[]{:S(2)}) collective-permute-start(bf16[1,2,1536]{2,1,0:T(2,128)(2,1)S(1)} %get-tuple-element.8), channel_id=1, source_target_pairs={{0,2},{2,4},{4,6},{6,8},{8,10},{10,12},{12,14},{1,3},{3,5},{5,7},{... | collective-permute-start | bytes 18440 | tf_op jit(solution)/shard_map/ppermute | solution.py:17
  66.7 0.0 copy-start.5
  66.7 1.3 collective-permute-start.1
  68.0 0.0 collective-permute-done
  68.0 0.8 fusion.36
  68.8 0.9 fusion.41
  69.7 1.2 constant_dynamic-update-slice_fusion
  70.9 1.3 collective-permute-done.1
  72.2 0.9 fusion.34
  73.1 0.9 fusion.40
  74.0 64.1 %all-gather.3.cloned.1.call-done = bf16[5,1536,384]{2,1,0:T(8,128)(2,1)} async-done(((bf16[5,192,384]{2,1,0:T(8,128)(2,1)}), bf16[5,1536,384]{2,1,0:T(8,128)(2,1)}) %all-gather.3.cloned.1.call-update) | async-done | bytes 5898256 | tf_op jit(solution)/shard_map/all_gather | solution.py:113
  138.1 0.0 copy-done.5
  138.1 5.1 %fusion.14 = bf16[1,128,384]{2,1,0:T(8,128)(2,1)} fusion(bf16[7680,384]{1,0:T(8,128)(2,1)} %bitcast.79, bf16[1,128,7680]{2,1,0:T(8,128)(2,1)} %fusion.40, bf16[1,128,1536]{2,1,0:T(8,128)(2,1)S(1)} %get-tuple-element.6, s32[]{:T(128)S(6)} %select_n.16, f32[384]{0:T(512)S(1)} %copy-done.5), kind=kOutput, calls=%fused_computation.11 | convolution fusion | flops 755171328 | bytes 8062468 | tf_op jit(solution)/shard_map/dot_general | solution.py:119
  (7 shorter events, 0.1 us)
Async XLA Ops:
  7.4 35.6 %copy-start = (bf16[512,1536]{1,0:T(8,128)(2,1)S(1)}, bf16[512,1536]{1,0:T(8,128)(2,1)}, u32[]{:S(2)}) copy-start(bf16[512,1536]{1,0:T(8,128)(2,1)} %param.14) | copy-start | bytes 4718596
  7.4 5.0 %copy-start.2 = (f32[1536]{0:T(1024)S(1)}, f32[1536]{0:T(1024)}, u32[]{:S(2)}) copy-start(f32[1536]{0:T(1024)} %param.10) | copy-start | bytes 18436
  7.4 31.7 %copy-start.1 = (bf16[1536,512]{1,0:T(8,128)(2,1)S(1)}, bf16[1536,512]{1,0:T(8,128)(2,1)}, u32[]{:S(2)}) copy-start(bf16[1536,512]{1,0:T(8,128)(2,1)} %param.11) | copy-start | bytes 4718596
  7.4 52.2 %all-reduce.3.cloned.1.call-start = ((), (), s32[]{:S(2)}) async-start(), calls=%async_computation | async-start | bytes 393216 | tf_op jit(solution)/shard_map/psum | solution.py:105
  11.4 28.2 %copy-start.4 = (f32[1,4,4,32]{3,2,1,0:T(4,128)S(1)}, f32[1,4,4,32]{3,2,1,0:T(4,128)}, u32[]{:S(2)}) copy-start(f32[1,4,4,32]{3,2,1,0:T(4,128)} %param.13) | copy-start | bytes 6148
  44.0 94.0 %all-gather.3.cloned.1.call-start = ((), (), s32[]{:S(2)}) async-start(), calls=%async_computation.1 | async-start | bytes 6635520 | tf_op jit(solution)/shard_map/all_gather | solution.py:113
  60.6 2.1 %copy-start.3 = (f32[1536]{0:T(1024)S(1)}, f32[1536]{0:T(1024)}, u32[]{:S(2)}) copy-start(f32[1536]{0:T(1024)} %param.15) | copy-start | bytes 18436
  63.0 5.0 %collective-permute-start = (bf16[1,2,1536]{2,1,0:T(2,128)(2,1)S(1)}, bf16[1,2,1536]{2,1,0:T(2,128)(2,1)S(1)}, u32[]{:S(2)}, u32[]{:S(2)}) collective-permute-start(bf16[1,2,1536]{2,1,0:T(2,128)(2,1)S(1)} %get-tuple-element.8), channel_id=1, source_target_pairs={{0,2},{2,4},{4,6},{6,8},{8,10},{10,12},{12,14},{1,3},{3,5},{5,7},{... | collective-permute-start | bytes 18440 | tf_op jit(solution)/shard_map/ppermute | solution.py:17
  66.7 71.4 %copy-start.5 = (f32[384]{0:T(512)S(1)}, f32[384]{0:T(512)}, u32[]{:S(2)}) copy-start(f32[384]{0:T(512)} %param.17) | copy-start | bytes 4612
  66.7 5.5 %collective-permute-start.1 = (bf16[1,2,1536]{2,1,0:T(2,128)(2,1)S(1)}, bf16[1,2,1536]{2,1,0:T(2,128)(2,1)S(1)}, u32[]{:S(2)}, u32[]{:S(2)}) collective-permute-start(bf16[1,2,1536]{2,1,0:T(2,128)(2,1)S(1)} %get-tuple-element.7), channel_id=1, source_target_pairs={{2,0},{4,2},{6,4},{8,6},{10,8},{12,10},{14,12},{3,1},{5,3},{7,5},{... | collective-permute-start | bytes 18440 | tf_op jit(solution)/shard_map/ppermute | solution.py:20
Sparse Core Ops, SparseCore 0:
  44.2 15.3 all-reduce.2
Sparse Core Ops, SparseCore 1:
  46.7 91.3 all-gather.2
where the time goes:
time: 151 us
  waiting for transfers between devices  81 us (54%)
  blocking collectives  25.2 us (17%)
  between operations  15 us (10%)
  matrix products  10.6 us (7%)
  other arithmetic  10.3 us (7%)
  starting transfers between devices  4.96 us (3%)
  local copies, waits for them, and re-layouts  3.61 us (2%)
    all_gather x1, waiting for transfers between devices, body(): piece = lax.all_gather(dec_weight, 'seq', axis=1, tiled=True)  64.1 us
    all_gather x1, blocking collectives, body(): piece = lax.all_gather(key_values, ('seq', 'section'), axis=1, tiled=True)  25.2 us
    psum x1, waiting for transfers between devices, body(): lax.psum(partial_value.astype(jnp.bfloat16), 'section').astype(jnp.float32)  15 us
    dot_general x1, matrix products, body(): jnp.dot(stacked, piece.reshape(KW * piece_rows, out_half), preferred_elem...  5.14 us
    unnamed x4, other arithmetic  3.74 us
    ppermute x1, starting transfers between devices, extended(): lax.ppermute(lax.slice_in_dim(block, block.shape[dim] - width, None, axis...  3.62 us
  transfers between devices with their start and end apart: 4, of which 3 were waited for; matrix products, arithmetic and copies ran while one was open for 5% of the time, Pallas kernels for 0%

commit v1 on v0

--- a/solution.py
+++ b/solution.py
@@ -3,6 +3,7 @@
 import jax.numpy as jnp
 from jax import lax
 from jax.sharding import PartitionSpec as P
+from jax.lax import axis_index, axis_size, ppermute
 
 HEAD = 128
 KW = 5
@@ -110,7 +111,29 @@
     activated = jax.nn.gelu(norm_scale(joined, dec_gain)).astype(jnp.bfloat16)
     padded = extended(activated, (("seq", 1),), KW // 2)
     out_half = dec_weight.shape[2]
-    piece = lax.all_gather(dec_weight, "seq", axis=1, tiled=True)
+    nd = axis_size("seq")
+    entries = []
+    c = 0
+    while c < nd:
+        entries.append((c, (c + 1) % nd))
+        c = c + 1
+    heap = []
+    c = 0
+    while c < nd:
+        heap.append((c, (c - 1) % nd))
+        c = c + 1
+    d_next, ready = ([dec_weight], [dec_weight])
+    for _ in range(nd // 2):
+        d_next.append(ppermute(d_next[-1], perm=entries, axis_name="seq"))
+    p = 0
+    while p < (nd - 1) // 2:
+        ready.append(ppermute(ready[-1], axis_name="seq", perm=heap))
+        p = p + 1
+    piece = jnp.roll(
+        jnp.concatenate([*d_next[::-1], *ready[1:]], axis=1),
+        (axis_index("seq") - nd // 2) * dec_weight.shape[1],
+        axis=1,
+    )
     piece_rows = piece.shape[1]
     stacked = jnp.concatenate(
         [padded[:, tap_index : tap_index + local_rows] for tap_index in range(KW)], axis=2

time: 151 us -> 181 us (1.20)
  local copies, waits for them, and re-layouts: 3.61 us -> 31.9 us
  starting transfers between devices: 4.96 us -> 14.1 us
  other arithmetic: 10.3 us -> 5.56 us
  matrix products: 10.6 us -> 6.96 us
  waiting for transfers between devices: 81 us -> 83.6 us
    all_gather x1 -> x0, waiting for transfers between devices: 64.1 us -> none  [body(): piece = lax.all_gather(dec_weight, 'seq', axis=1, tiled=True)]
    ppermute x0 -> x7, waiting for transfers between devices: none -> 56.8 us  [the longest x3 37.7 us: body(): ready.append(ppermute(ready[-1], axis_name='seq', perm=heap))]
    unnamed x13 -> x22, local copies, waits for them, and re-layouts: 0.34 us -> 23.7 us
    ppermute x1, waiting for transfers between devices: 0.01 us -> 11.7 us  [extended(): lax.ppermute(lax.slice_in_dim(block, block.shape[dim] - width, None, axis...]
    ppermute x0 -> x7, starting transfers between devices: none -> 9.56 us  [the longest x3 4.84 us: body(): ready.append(ppermute(ready[-1], axis_name='seq', perm=heap))]
    dynamic_slice x0 -> x1, local copies, waits for them, and re-layouts: none -> 4.16 us  [body(): jnp.roll(jnp.concatenate([*d_next[::-1], *ready[1:]], axis=1), (axis_inde...]
    dot_general x1, matrix products: 5.14 us -> 1.9 us  [body(): jnp.dot(stacked, piece.reshape(KW * piece_rows, out_half), preferred_elem...]
    unnamed x4, other arithmetic: 3.74 us -> 0.69 us
  transfers between devices with their start and end apart: 4 -> 10, of which waited for: 3 -> 6; matrix products, arithmetic and copies ran while one was open for 5% -> 14% of each run, Pallas kernels for 0% -> 0%
where the time goes in v1:
time: 181 us
  waiting for transfers between devices  83.6 us (46%)
  local copies, waits for them, and re-layouts  31.9 us (18%)
  blocking collectives  25 us (14%)
  starting transfers between devices  14.1 us (8%)
  between operations  13.7 us (8%)
  matrix products  6.96 us (4%)
  other arithmetic  5.56 us (3%)
    ppermute x3, waiting for transfers between devices, body(): ready.append(ppermute(ready[-1], axis_name='seq', perm=heap))  37.7 us
    all_gather x1, blocking collectives, body(): piece = lax.all_gather(key_values, ('seq', 'section'), axis=1, tiled=True)  25 us
    unnamed x22, local copies, waits for them, and re-layouts  23.7 us
    ppermute x4, waiting for transfers between devices, body(): d_next.append(ppermute(d_next[-1], perm=entries, axis_name='seq'))  19.2 us
    psum x1, waiting for transfers between devices, body(): lax.psum(partial_value.astype(jnp.bfloat16), 'section').astype(jnp.float32)  15.1 us
    ppermute x1, waiting for transfers between devices, extended(): lax.ppermute(lax.slice_in_dim(block, block.shape[dim] - width, None, axis...  11.7 us
    ppermute x3, starting transfers between devices, body(): ready.append(ppermute(ready[-1], axis_name='seq', perm=heap))  4.84 us
    ppermute x4, starting transfers between devices, body(): d_next.append(ppermute(d_next[-1], perm=entries, axis_name='seq'))  4.72 us
  transfers between devices with their start and end apart: 10, of which 6 were waited for; matrix products, arithmetic and copies ran while one was open for 14% of the time, Pallas kernels for 0%

profile of v1, /device:TPU:0, one launch (start us, length us, event | category | flops | bytes accessed | tf_op | source)
XLA Modules:
  0.0 180.8 jit_solution(9574251749423127641)
XLA Ops:
  6.5 2.9 %collective-permute-start.2 = (bf16[5,192,384]{2,1,0:T(8,128)(2,1)}, bf16[5,192,384]{2,1,0:T(8,128)(2,1)}, u32[]{:S(2)}, u32[]{:S(2)}) collective-permute-start(bf16[5,192,384]{2,1,0:T(8,128)(2,1)} %param.16), channel_id=1, source_target_pairs={{0,2},{2,4},{4,6},{6,8},{8,10},{10,12},{12,14},{14,0},{1,3},{3,5},... | collective-permute-start | bytes 2211848 | tf_op jit(solution)/shard_map/ppermute | solution.py:127
  9.5 1.1 reshape.220
  10.6 1.0 reduce_max.18
  11.7 0.1 fusion.37
  11.8 0.8 convert_bitcast_fusion
  12.6 0.7 broadcast_in_dim.29
  13.3 0.1 copy.16
  13.4 0.1 broadcast_in_dim.31
  13.5 0.1 slice.41
  13.6 0.3 copy.19
  13.9 0.1 dynamic-slice.1
  14.0 1.9 %fusion.19 = bf16[8,4,8,128]{3,2,1,0:T(8,128)(2,1)S(1)} fusion(bf16[1536,512]{1,0:T(8,128)(2,1)} %param.11, bf16[64,1536]{1,0:T(8,128)(2,1)S(1)} %reduce_max.18, f32[1536]{0:T(1024)} %param.10, f32[64]{0:T(128)S(1)} %add_rsqrt_fusion.1), kind=kOutput, calls=%fused_computation.16 | convolution fusion | flops 101089280 | bytes 1841408 | tf_op jit(solution)/shard_map/dot_general | solution.py:49
  15.9 1.5 convolution_convert_fusion.2
  17.4 25.0 %all-gather = bf16[512,256]{1,0:T(8,128)(2,1)S(1)} all-gather(bf16[32,256]{1,0:T(8,128)(2,1)S(1)} %convolution_convert_fusion.2), channel_id=2, replica_groups=mesh['groups'=2,'seq'=8,'section'=2] {'seq','section'}, dimensions={0}, use_global_device_ids=true | all-gather | bytes 278528 | tf_op jit(solution)/shard_map/all_gather | solution.py:63
  42.4 0.3 fusion.63
  42.7 0.2 fusion.31
  42.9 0.3 fusion.20
  43.2 0.1 copy.18
  43.3 1.1 fusion
  44.4 0.0 all-reduce.3.cloned.1.call-update
  44.4 0.4 collective-permute-start.6
  44.8 15.1 %all-reduce.3.cloned.1.call-done = bf16[1,64,1536]{2,1,0:T(8,128)(2,1)} async-done(((bf16[1,64,1536]{2,1,0:T(8,128)(2,1)}), bf16[1,64,1536]{2,1,0:T(8,128)(2,1)}) %all-reduce.3.cloned.1.call-update) | async-done | bytes 196624 | tf_op jit(solution)/shard_map/psum | solution.py:106
  59.9 1.0 fusion.46
  60.9 0.3 broadcast_in_dim.34
  61.2 0.5 convert_element_type.120
  61.7 0.0 collective-permute-done.2
  61.8 1.8 collective-permute-start.3
  63.5 1.2 fusion.21
  64.7 0.4 fusion.25
  65.1 18.4 %collective-permute-done.3 = bf16[5,192,384]{2,1,0:T(8,128)(2,1)} collective-permute-done((bf16[5,192,384]{2,1,0:T(8,128)(2,1)}, bf16[5,192,384]{2,1,0:T(8,128)(2,1)}, u32[]{:S(2)}, u32[]{:S(2)}) %collective-permute-start.3) | collective-permute-done | bytes 737312 | tf_op jit(solution)/shard_map/ppermute | solution.py:127
  83.6 0.0 collective-permute-start.4
  83.6 3.3 %collective-permute-start = (bf16[1,2,1536]{2,1,0:T(2,128)(2,1)S(1)}, bf16[1,2,1536]{2,1,0:T(2,128)(2,1)S(1)}, u32[]{:S(2)}, u32[]{:S(2)}) collective-permute-start(bf16[1,2,1536]{2,1,0:T(2,128)(2,1)S(1)} %get-tuple-element.8), channel_id=1, source_target_pairs={{0,2},{2,4},{4,6},{6,8},{8,10},{10,12},{12,14},{1,3},{3,5},{5,7},{... | collective-permute-start | bytes 18440 | tf_op jit(solution)/shard_map/ppermute | solution.py:18
  86.9 1.3 collective-permute-start.1
  88.2 11.7 %collective-permute-done = bf16[1,2,1536]{2,1,0:T(2,128)(2,1)S(1)} collective-permute-done((bf16[1,2,1536]{2,1,0:T(2,128)(2,1)S(1)}, bf16[1,2,1536]{2,1,0:T(2,128)(2,1)S(1)}, u32[]{:S(2)}, u32[]{:S(2)}) %collective-permute-start) | collective-permute-done | bytes 6176 | tf_op jit(solution)/shard_map/ppermute | solution.py:18
  99.8 0.1 fusion.36
  99.9 0.1 fusion.41
  100.1 3.8 %collective-permute-start.7 = (bf16[5,192,384]{2,1,0:T(8,128)(2,1)}, bf16[5,192,384]{2,1,0:T(8,128)(2,1)S(1)}, u32[]{:S(2)}, u32[]{:S(2)}) collective-permute-start(bf16[5,192,384]{2,1,0:T(8,128)(2,1)} %collective-permute-done.6), channel_id=1, source_target_pairs={{0,14},{2,0},{4,2},{6,4},{8,6},{10,8},{12,10},{14,12},{1,15},{3,1}... | collective-permute-start | bytes 2211848 | tf_op jit(solution)/shard_map/ppermute | solution.py:130
  103.8 0.7 collective-permute-done.4
  104.5 0.4 constant_dynamic-update-slice_fusion
  104.9 0.0 collective-permute-done.1
  104.9 0.1 fusion.34
  105.0 0.1 fusion.40
  105.2 31.0 %collective-permute-done.7 = bf16[5,192,384]{2,1,0:T(8,128)(2,1)S(1)} collective-permute-done((bf16[5,192,384]{2,1,0:T(8,128)(2,1)}, bf16[5,192,384]{2,1,0:T(8,128)(2,1)S(1)}, u32[]{:S(2)}, u32[]{:S(2)}) %collective-permute-start.7) | collective-permute-done | bytes 737312 | tf_op jit(solution)/shard_map/ppermute | solution.py:130
  136.2 0.7 collective-permute-start.8
  136.8 0.0 collective-permute-done.5
  136.8 1.0 constant_dynamic-update-slice_fusion.16
  137.8 1.0 constant_dynamic-update-slice_fusion.15
  138.7 2.1 %constant_dynamic-update-slice_fusion.14 = bf16[5,3072,384]{2,1,0:T(8,128)(2,1)} fusion(bf16[5,3072,384]{2,1,0:T(8,128)(2,1)} %constant_dynamic-update-slice_fusion.15, bf16[5,192,384]{2,1,0:T(8,128)(2,1)} %collective-permute-done.3), kind=kLoop, calls=%fused_computation.87 | loop fusion | bytes 1474560
  140.8 2.1 %constant_dynamic-update-slice_fusion.13 = bf16[5,3072,384]{2,1,0:T(8,128)(2,1)} fusion(bf16[5,3072,384]{2,1,0:T(8,128)(2,1)} %constant_dynamic-update-slice_fusion.14, bf16[5,192,384]{2,1,0:T(8,128)(2,1)} %collective-permute-done.2), kind=kLoop, calls=%fused_computation.86 | loop fusion | bytes 1474560
  142.9 2.1 %constant_dynamic-update-slice_fusion.12 = bf16[5,3072,384]{2,1,0:T(8,128)(2,1)} fusion(bf16[5,3072,384]{2,1,0:T(8,128)(2,1)} %constant_dynamic-update-slice_fusion.13, bf16[5,192,384]{2,1,0:T(8,128)(2,1)} %param.16), kind=kLoop, calls=%fused_computation.85 | loop fusion | bytes 1474560
  145.0 2.1 %constant_dynamic-update-slice_fusion.11 = bf16[5,3072,384]{2,1,0:T(8,128)(2,1)} fusion(bf16[5,3072,384]{2,1,0:T(8,128)(2,1)} %constant_dynamic-update-slice_fusion.12, bf16[5,192,384]{2,1,0:T(8,128)(2,1)} %collective-permute-done.6), kind=kLoop, calls=%fused_computation.84 | loop fusion | bytes 1474560
  147.0 0.9 constant_dynamic-update-slice_fusion.10
  148.0 6.7 %collective-permute-done.8 = bf16[5,192,384]{2,1,0:T(8,128)(2,1)S(1)} collective-permute-done((bf16[5,192,384]{2,1,0:T(8,128)(2,1)S(1)}, bf16[5,192,384]{2,1,0:T(8,128)(2,1)S(1)}, u32[]{:S(2)}, u32[]{:S(2)}) %collective-permute-start.8) | collective-permute-done | bytes 737312 | tf_op jit(solution)/shard_map/ppermute | solution.py:130
  154.6 1.0 constant_dynamic-update-slice_fusion.9
  155.6 1.0 constant_dynamic-update-slice_fusion.8
  156.6 1.0 constant_dynamic-update-slice_fusion.7
  157.6 2.1 %constant_dynamic-update-slice_fusion.6 = bf16[5,3072,384]{2,1,0:T(8,128)(2,1)} fusion(bf16[5,3072,384]{2,1,0:T(8,128)(2,1)} %constant_dynamic-update-slice_fusion.7, bf16[5,192,384]{2,1,0:T(8,128)(2,1)} %collective-permute-done.3), kind=kLoop, calls=%fused_computation.79 | loop fusion | bytes 1474560
  159.7 2.1 %constant_dynamic-update-slice_fusion.5 = bf16[5,3072,384]{2,1,0:T(8,128)(2,1)} fusion(bf16[5,3072,384]{2,1,0:T(8,128)(2,1)} %constant_dynamic-update-slice_fusion.6, bf16[5,192,384]{2,1,0:T(8,128)(2,1)} %collective-permute-done.2), kind=kLoop, calls=%fused_computation.78 | loop fusion | bytes 1474560
  161.8 2.1 %constant_dynamic-update-slice_fusion.4 = bf16[5,3072,384]{2,1,0:T(8,128)(2,1)} fusion(bf16[5,3072,384]{2,1,0:T(8,128)(2,1)} %constant_dynamic-update-slice_fusion.5, bf16[5,192,384]{2,1,0:T(8,128)(2,1)} %param.16), kind=kLoop, calls=%fused_computation.77 | loop fusion | bytes 1474560
  163.8 2.1 %constant_dynamic-update-slice_fusion.3 = bf16[5,3072,384]{2,1,0:T(8,128)(2,1)} fusion(bf16[5,3072,384]{2,1,0:T(8,128)(2,1)} %constant_dynamic-update-slice_fusion.4, bf16[5,192,384]{2,1,0:T(8,128)(2,1)} %collective-permute-done.6), kind=kLoop, calls=%fused_computation.76 | loop fusion | bytes 1474560
  165.9 1.0 constant_dynamic-update-slice_fusion.2
  166.9 1.0 constant_dynamic-update-slice_fusion.1
  167.8 4.2 %constant_dynamic-slice_fusion = bf16[5,1536,384]{2,1,0:T(8,128)(2,1)S(1)} fusion(bf16[5,3072,384]{2,1,0:T(8,128)(2,1)} %constant_dynamic-update-slice_fusion.1, s32[]{:T(128)S(6)} %select_n.29), kind=kLoop, calls=%fused_computation.92 | loop fusion | bytes 11796484 | tf_op jit(solution)/shard_map/jit(_roll_dynamic)/dynamic_slice | solution.py:132
  172.0 1.9 %fusion.14 = bf16[1,128,384]{2,1,0:T(8,128)(2,1)} fusion(bf16[7680,384]{1,0:T(8,128)(2,1)S(1)} %bitcast.79, bf16[1,128,7680]{2,1,0:T(8,128)(2,1)S(1)} %fusion.40, bf16[1,128,1536]{2,1,0:T(8,128)(2,1)S(1)} %get-tuple-element.6, s32[]{:T(128)S(6)} %select_n.30, f32[384]{0:T(512)S(1)} %copy-done.2), kind=kOutput, calls=%fused_computation.11 | convolution fusion | flops 755171328 | bytes 8062468 | tf_op jit(solution)/shard_map/dot_general | solution.py:142
  (15 shorter events, 0.1 us)
Async XLA Ops:
  6.5 36.8 %copy-start = (bf16[512,1536]{1,0:T(8,128)(2,1)S(1)}, bf16[512,1536]{1,0:T(8,128)(2,1)}, u32[]{:S(2)}) copy-start(bf16[512,1536]{1,0:T(8,128)(2,1)} %param.14) | copy-start | bytes 4718596
  6.5 58.2 %copy-start.1 = (f32[1536]{0:T(1024)S(1)}, f32[1536]{0:T(1024)}, u32[]{:S(2)}) copy-start(f32[1536]{0:T(1024)} %param.15) | copy-start | bytes 18436
  6.5 53.4 %all-reduce.3.cloned.1.call-start = ((), (), s32[]{:S(2)}) async-start(), calls=%async_computation | async-start | bytes 393216 | tf_op jit(solution)/shard_map/psum | solution.py:106
  6.5 55.2 %collective-permute-start.2 = (bf16[5,192,384]{2,1,0:T(8,128)(2,1)}, bf16[5,192,384]{2,1,0:T(8,128)(2,1)}, u32[]{:S(2)}, u32[]{:S(2)}) collective-permute-start(bf16[5,192,384]{2,1,0:T(8,128)(2,1)} %param.16), channel_id=1, source_target_pairs={{0,2},{2,4},{4,6},{6,8},{8,10},{10,12},{12,14},{14,0},{1,3},{3,5},... | collective-permute-start | bytes 2211848 | tf_op jit(solution)/shard_map/ppermute | solution.py:127
  44.4 55.6 %collective-permute-start.6 = (bf16[5,192,384]{2,1,0:T(8,128)(2,1)}, bf16[5,192,384]{2,1,0:T(8,128)(2,1)}, u32[]{:S(2)}, u32[]{:S(2)}) collective-permute-start(bf16[5,192,384]{2,1,0:T(8,128)(2,1)} %param.16), channel_id=1, source_target_pairs={{0,14},{2,0},{4,2},{6,4},{8,6},{10,8},{12,10},{14,12},{1,15},{3,1}... | collective-permute-start | bytes 2211848 | tf_op jit(solution)/shard_map/ppermute | solution.py:130
  61.8 21.8 %collective-permute-start.3 = (bf16[5,192,384]{2,1,0:T(8,128)(2,1)}, bf16[5,192,384]{2,1,0:T(8,128)(2,1)}, u32[]{:S(2)}, u32[]{:S(2)}) collective-permute-start(bf16[5,192,384]{2,1,0:T(8,128)(2,1)} %collective-permute-done.2), channel_id=1, source_target_pairs={{0,2},{2,4},{4,6},{6,8},{8,10},{10,12},{12,14},{14,0},{1,3},{3,5},... | collective-permute-start | bytes 2211848 | tf_op jit(solution)/shard_map/ppermute | solution.py:127
  83.6 21.0 %collective-permute-start.4 = (bf16[5,192,384]{2,1,0:T(8,128)(2,1)}, bf16[5,192,384]{2,1,0:T(8,128)(2,1)S(1)}, u32[]{:S(2)}, u32[]{:S(2)}) collective-permute-start(bf16[5,192,384]{2,1,0:T(8,128)(2,1)} %collective-permute-done.3), channel_id=1, source_target_pairs={{0,2},{2,4},{4,6},{6,8},{8,10},{10,12},{12,14},{14,0},{1,3},{3,5},... | collective-permute-start | bytes 2211848 | tf_op jit(solution)/shard_map/ppermute | solution.py:127
  83.6 16.2 %collective-permute-start = (bf16[1,2,1536]{2,1,0:T(2,128)(2,1)S(1)}, bf16[1,2,1536]{2,1,0:T(2,128)(2,1)S(1)}, u32[]{:S(2)}, u32[]{:S(2)}) collective-permute-start(bf16[1,2,1536]{2,1,0:T(2,128)(2,1)S(1)} %get-tuple-element.8), channel_id=1, source_target_pairs={{0,2},{2,4},{4,6},{6,8},{8,10},{10,12},{12,14},{1,3},{3,5},{5,7},{... | collective-permute-start | bytes 18440 | tf_op jit(solution)/shard_map/ppermute | solution.py:18
  86.9 18.1 %collective-permute-start.1 = (bf16[1,2,1536]{2,1,0:T(2,128)(2,1)S(1)}, bf16[1,2,1536]{2,1,0:T(2,128)(2,1)S(1)}, u32[]{:S(2)}, u32[]{:S(2)}) collective-permute-start(bf16[1,2,1536]{2,1,0:T(2,128)(2,1)S(1)} %get-tuple-element.7), channel_id=1, source_target_pairs={{2,0},{4,2},{6,4},{8,6},{10,8},{12,10},{14,12},{3,1},{5,3},{7,5},{... | collective-permute-start | bytes 18440 | tf_op jit(solution)/shard_map/ppermute | solution.py:21
  100.1 36.1 %collective-permute-start.7 = (bf16[5,192,384]{2,1,0:T(8,128)(2,1)}, bf16[5,192,384]{2,1,0:T(8,128)(2,1)S(1)}, u32[]{:S(2)}, u32[]{:S(2)}) collective-permute-start(bf16[5,192,384]{2,1,0:T(8,128)(2,1)} %collective-permute-done.6), channel_id=1, source_target_pairs={{0,14},{2,0},{4,2},{6,4},{8,6},{10,8},{12,10},{14,12},{1,15},{3,1}... | collective-permute-start | bytes 2211848 | tf_op jit(solution)/shard_map/ppermute | solution.py:130
  104.5 32.3 %collective-permute-start.5 = (bf16[5,192,384]{2,1,0:T(8,128)(2,1)S(1)}, bf16[5,192,384]{2,1,0:T(8,128)(2,1)S(1)}, u32[]{:S(2)}, u32[]{:S(2)}) collective-permute-start(bf16[5,192,384]{2,1,0:T(8,128)(2,1)S(1)} %collective-permute-done.4), channel_id=1, source_target_pairs={{0,2},{2,4},{4,6},{6,8},{8,10},{10,12},{12,14},{14,0},{1,3},{3,5},... | collective-permute-start | bytes 2211848 | tf_op jit(solution)/shard_map/ppermute | solution.py:127
  136.2 18.5 %collective-permute-start.8 = (bf16[5,192,384]{2,1,0:T(8,128)(2,1)S(1)}, bf16[5,192,384]{2,1,0:T(8,128)(2,1)S(1)}, u32[]{:S(2)}, u32[]{:S(2)}) collective-permute-start(bf16[5,192,384]{2,1,0:T(8,128)(2,1)S(1)} %collective-permute-done.7), channel_id=1, source_target_pairs={{0,14},{2,0},{4,2},{6,4},{8,6},{10,8},{12,10},{14,12},{1,15},{3,1}... | collective-permute-start | bytes 2211848 | tf_op jit(solution)/shard_map/ppermute | solution.py:130
  155.6 16.4 %copy-start.2 = (f32[384]{0:T(512)S(1)}, f32[384]{0:T(512)}, u32[]{:S(2)}) copy-start(f32[384]{0:T(512)} %param.17) | copy-start | bytes 4612
Sparse Core Ops, SparseCore 0:
  44.5 15.3 all-reduce.2
